TPU v7x, 32 devices: a whole 2x2x4 slice. The times are simulated.
32 devices in a mesh: groups: 1, ex: 32 (over z, y, x, core).
Axes of the slice: x: 2, y: 2, z: 4, core: 2. Of those that a mesh axis runs over, the one named last changes fastest.
Arguments:
- residual_in: bfloat16 [2, 1024, 2048], P(None, ('groups', 'ex')), may hold values from -6 to 6
- queries: bfloat16 [2, 1024, 2048], P(None, ('groups', 'ex')), may hold values from -100 to 100
- new_entries: bfloat16 [2, 1024, 2, 256], P(None, ('groups', 'ex')), may hold values from -6 to 6
- cache_keys: bfloat16 [2, 1024, 64, 256], P(None, ('groups', 'ex')), may hold values from -4.5 to 4.5
- cache_values: bfloat16 [2, 1024, 64, 256], P(None, ('groups', 'ex')), may hold values from -6 to 6
- lengths: int32 [2, 1024], P(None, ('groups', 'ex')), may hold values from 2 to 64, as said below
- skip_flags: int32 [2, 1024], P(None, ('groups', 'ex')), may hold values 0 or 1
- expert_ids: int32 [2, 1024, 8], P(None, ('groups', 'ex')), may hold values from 0 to 31, all different within a row; in each aligned block of 32 rows (0 to 31, 32 to 63, ..., all dimensions but the last counted through in order) at most 16 rows name the same one
- gate_weights: float32 [2, 1024, 8], P(None, ('groups', 'ex')), may hold values from 0.1 to 1
- norm_gain: float32 [2048], replicated, may hold values from 0.1 to 1.9
- gate_proj: bfloat16 [32, 2048, 768], P('ex'), may hold values from -0.125 to 0.125
- up_proj: bfloat16 [32, 2048, 768], P('ex'), may hold values from -0.125 to 0.125
- down_proj: bfloat16 [32, 768, 2048], P('ex'), may hold values from -0.21875 to 0.21875
Outputs:
- layer_out: bfloat16 [2, 1024, 2048], P(None, ('groups', 'ex'))
Inputs may be any that keep to these rules, and one draw needn't show every extreme that they name: `expert_ids`: in each micro-batch, the 32 rows of one device name any one expert at most 16 times; each row names 8 different experts. `lengths`: in each micro-batch, every device's block of 32 rows holds a row of length 64.
All inputs are finite; a program needn't handle non-finite values. No bound on the sum of `skip_flags` on one device may be relied on, other than what follows from the above.
Results may differ from a plain program's by a relative error of at most 0.0065.
Values may be sent and summed in bfloat16 or wider, within the bound.
A program may use at most 128 MiB of HBM per device.

v0:
```python
import jax
import jax.numpy as jnp
from jax import lax
from jax.sharding import PartitionSpec as P

HEADS = 16
KEY_VALUE_HEADS = 2
HEAD_WIDTH = 128


def attend(queries, entries, keys, value_entries, lengths):
    token_row_count = queries.shape[0]
    cache_slot_index = keys.shape[1]
    group = HEADS // KEY_VALUE_HEADS
    scale = HEAD_WIDTH ** (-0.5)
    qvec = queries.reshape(token_row_count, KEY_VALUE_HEADS, group, HEAD_WIDTH)
    kmat = keys.reshape(token_row_count, cache_slot_index, KEY_VALUE_HEADS, HEAD_WIDTH)
    value_matrix = value_entries.reshape(
        token_row_count, cache_slot_index, KEY_VALUE_HEADS, HEAD_WIDTH
    )
    own_key = entries[:, 0].reshape(token_row_count, KEY_VALUE_HEADS, HEAD_WIDTH)
    self_value_vector = entries[:, 1].reshape(token_row_count, KEY_VALUE_HEADS, HEAD_WIDTH)
    cache_scores = (
        jnp.einsum("rkgd,rlkd->rkgl", qvec, kmat, preferred_element_type=jnp.float32) * scale
    )
    own_scores = (
        jnp.einsum("rkgd,rkd->rkg", qvec, own_key, preferred_element_type=jnp.float32) * scale
    )
    live = (jnp.arange(cache_slot_index, dtype=jnp.int32)[None, :] < lengths[:, None])[
        :, None, None, :
    ]
    cache_scores = jnp.where(live, cache_scores, -1e30)
    top = jnp.maximum(jnp.max(cache_scores, axis=-1), own_scores)
    cache_p = jnp.where(live, jnp.exp(cache_scores - top[..., None]), 0.0)
    own_p = jnp.exp(own_scores - top)
    total = jnp.sum(cache_p, axis=-1) + own_p
    cache_weight_part = (cache_p / total[..., None]).astype(jnp.bfloat16)
    self_weight_part = (own_p / total).astype(jnp.bfloat16)
    blended_output = jnp.einsum(
        "xtio,xotw->xtiw", cache_weight_part, value_matrix, preferred_element_type=jnp.float32
    )
    blended_output = blended_output + self_weight_part[..., None].astype(
        jnp.float32
    ) * self_value_vector[:, :, None, :].astype(jnp.float32)
    return blended_output.reshape(token_row_count, HEADS * HEAD_WIDTH).astype(jnp.bfloat16)


def prepare(residual, queries, entries, keys, value_entries, lengths, norm_gain):
    attended = attend(queries, entries, keys, value_entries, lengths)
    stream = residual.astype(jnp.float32) + attended.astype(jnp.float32)
    meansq = jnp.mean(stream * stream, axis=-1, keepdims=True)
    normed = (stream / jnp.sqrt(meansq + 1e-06) * norm_gain[None, :]).astype(jnp.bfloat16)
    return (stream, normed)


def combine_table(expert_ids, gate_weights, experts):
    gates = gate_weights / jnp.sum(gate_weights, axis=-1, keepdims=True)
    named = expert_ids[..., None] == jnp.arange(experts, dtype=jnp.int32)
    return jnp.sum(jnp.where(named, gates[..., None], 0.0), axis=-2)


def expert_rows(flat, gate_proj, up_proj, down_proj):
    gate = jnp.dot(flat, gate_proj[0], preferred_element_type=jnp.float32)
    upper = jnp.dot(flat, up_proj[0], preferred_element_type=jnp.float32)
    hidden = (jax.nn.silu(gate) * upper).astype(jnp.bfloat16)
    return jnp.dot(hidden, down_proj[0], preferred_element_type=jnp.float32).astype(jnp.bfloat16)


def on_device(
    residual_in,
    queries,
    new_entries,
    cache_keys,
    cache_values,
    lengths,
    skip_flags,
    expert_ids,
    gate_weights,
    norm_gain,
    gate_proj,
    up_proj,
    down_proj,
):
    micro_count, rows, width = residual_in.shape
    shards = lax.axis_size("ex")
    experts = gate_proj.shape[0] * shards
    table = combine_table(expert_ids, gate_weights, experts)
    mine = lax.all_to_all(table, "ex", split_axis=2, concat_axis=1, tiled=True)
    results = []
    for micro in range(micro_count):
        stream, normed = prepare(
            residual_in[micro],
            queries[micro],
            new_entries[micro],
            cache_keys[micro],
            cache_values[micro],
            lengths[micro],
            norm_gain,
        )
        gathered = lax.all_gather(normed, "ex", axis=0, tiled=True)
        out = expert_rows(gathered, gate_proj, up_proj, down_proj)
        partial = (mine[micro] * out.astype(jnp.float32)).astype(jnp.bfloat16)
        mixture = lax.psum_scatter(partial, "ex", scatter_dimension=0, tiled=True)
        merged = (stream + mixture.astype(jnp.float32)).astype(jnp.bfloat16)
        results.append(jnp.where(skip_flags[micro][:, None] == 1, residual_in[micro], merged))
    return jnp.stack(results, axis=0)


def solution(mesh):
    in_specs = (
        P(None, ("groups", "ex"), None),
        P(None, ("groups", "ex"), None),
        P(None, ("groups", "ex"), None, None),
        P(None, ("groups", "ex"), None, None),
        P(None, ("groups", "ex"), None, None),
        P(None, ("groups", "ex")),
        P(None, ("groups", "ex")),
        P(None, ("groups", "ex"), None),
        P(None, ("groups", "ex"), None),
        P(),
        P("ex", None, None),
        P("ex", None, None),
        P("ex", None, None),
    )
    out_specs = P(None, ("groups", "ex"), None)
    return jax.shard_map(
        on_device, mesh=mesh, in_specs=in_specs, out_specs=out_specs, check_vma=False
    )
```

profile of v0, /device:TPU:0, one launch (start us, length us, event | category | flops | bytes accessed | tf_op | source)
XLA Modules:
  0.0 465.2 jit_solution(1728249540020639107)
XLA Ops:
  6.5 0.8 slice_bitcast_fusion.9
  7.4 1.8 slice_bitcast_fusion.1
  9.2 3.1 fusion.54
  12.3 2.2 reshape_squeeze.29
  14.5 2.6 fusion.57
  17.1 0.8 copy.59
  17.9 1.4 slice_bitcast_fusion.5
  20.0 0.8 fusion.43
  20.8 0.8 copy.68
  23.5 1.5 slice_convert_fusion
  24.9 3.1 fusion.55
  28.0 2.2 reshape_squeeze.31
  30.2 0.9 copy.69
  31.1 2.1 reshape_squeeze.25
  33.3 1.6 fusion.42
  34.9 3.2 fusion.56
  38.1 0.8 copy.49
  38.9 0.8 copy.66
  39.8 1.2 fusion.28
  41.3 2.1 reshape_squeeze.27
  43.5 1.8 fusion.19
  46.7 0.9 multiply_convert_fusion.5
  48.9 14.3 %all_to_all.15 = f32[2,32,32]{1,0,2:T(2,128)S(1)} all-to-all(f32[2,32,32]{1,0,2:T(2,128)S(1)} %copy.57), channel_id=1, replica_groups=mesh['groups'=1,'ex'=32] {'ex'}, dimensions={2} | all-to-all | bytes 16384 | tf_op jit(solution)/shard_map/all_to_all | solution.py:88
  63.4 49.0 %all-gather.5.cloned.1.call-done = bf16[1024,2048]{1,0:T(8,128)(2,1)} async-done(((bf16[32,2048]{1,0:T(8,128)(2,1)}), bf16[1024,2048]{1,0:T(8,128)(2,1)}) %all-gather.5.cloned.1.call-update) | async-done | bytes 4194320 | tf_op jit(solution)/shard_map/all_gather | solution.py:100
  112.4 8.2 %fusion.2 = f32[1024,768]{1,0:T(8,128)} fusion(bf16[1024,2048]{1,0:T(8,128)(2,1)} %all-gather.5.cloned.1.call-done, bf16[1,2048,768]{2,1,0:T(8,128)(2,1)} %param.24), kind=kOutput, calls=%fused_computation.4 | convolution fusion | flops 3221225472 | bytes 10485760 | tf_op jit(solution)/shard_map/dot_general | solution.py:64
  120.6 12.5 %multiply_convert_fusion = bf16[1024,2048]{1,0:T(8,128)(2,1)} fusion(f32[1024]{0:T(1024)S(1)} %mul.109, bf16[1,768,2048]{2,1,0:T(8,128)(2,1)S(1)} %copy-done, f32[1024,768]{1,0:T(8,128)} %fusion.2, bf16[1024,2048]{1,0:T(8,128)(2,1)} %all-gather.5.cloned.1.call-done, bf16[1,2048,768]{2,1,0:T(8,128)(2,1)} %param.23), kind=kOutput, calls=%fused_computation | convolution fusion | flops 6455558144 | bytes 17829888 | tf_op jit(solution)/shard_map/dot_general | solution.py:66
  133.4 42.5 %all-gather.3.cloned.1.call-done = bf16[1024,2048]{1,0:T(8,128)(2,1)} async-done(((bf16[32,2048]{1,0:T(8,128)(2,1)}), bf16[1024,2048]{1,0:T(8,128)(2,1)}) %all-gather.3.cloned.1.call-update) | async-done | bytes 4194320 | tf_op jit(solution)/shard_map/all_gather | solution.py:100
  175.9 8.2 %fusion.4 = f32[1024,768]{1,0:T(8,128)} fusion(bf16[1024,2048]{1,0:T(8,128)(2,1)} %all-gather.3.cloned.1.call-done, bf16[1,2048,768]{2,1,0:T(8,128)(2,1)} %param.24), kind=kOutput, calls=%fused_computation.6 | convolution fusion | flops 3221225472 | bytes 10485760 | tf_op jit(solution)/shard_map/dot_general | solution.py:64
  184.1 12.3 %multiply_convert_fusion.1 = bf16[1024,2048]{1,0:T(8,128)(2,1)} fusion(f32[1024]{0:T(1024)S(1)} %mul.96, bf16[1,768,2048]{2,1,0:T(8,128)(2,1)S(1)} %copy-done, f32[1024,768]{1,0:T(8,128)} %fusion.4, bf16[1024,2048]{1,0:T(8,128)(2,1)} %all-gather.3.cloned.1.call-done, bf16[1,2048,768]{2,1,0:T(8,128)(2,1)} %param.23), kind=kOutput, calls=%fused_computation.1 | convolution fusion | flops 6455558144 | bytes 17829888 | tf_op jit(solution)/shard_map/dot_general | solution.py:66
  197.1 120.5 %reduce-scatter.5.cloned.1.call-done = bf16[32,2048]{1,0:T(8,128)(2,1)} async-done(((bf16[1024,2048]{1,0:T(8,128)(2,1)}), bf16[32,2048]{1,0:T(8,128)(2,1)}) %reduce-scatter.5.cloned.1.call-update) | async-done | bytes 131088 | tf_op jit(solution)/shard_map/reduce_scatter | solution.py:103
  317.6 139.0 %reduce-scatter.3.cloned.1.call-done = bf16[32,2048]{1,0:T(8,128)(2,1)} async-done(((bf16[1024,2048]{1,0:T(8,128)(2,1)}), bf16[32,2048]{1,0:T(8,128)(2,1)}) %reduce-scatter.3.cloned.1.call-update) | async-done | bytes 131088 | tf_op jit(solution)/shard_map/reduce_scatter | solution.py:103
  456.6 2.1 fusion.31
  (64 shorter events, 6.6 us)
Async XLA Ops:
  6.5 114.1 %copy-start = (bf16[1,768,2048]{2,1,0:T(8,128)(2,1)S(1)}, bf16[1,768,2048]{2,1,0:T(8,128)(2,1)}, u32[]{:S(2)}) copy-start(bf16[1,768,2048]{2,1,0:T(8,128)(2,1)} %param.25) | copy-start | bytes 9437188
  6.5 105.9 %all-gather.5.cloned.1.call-start = ((), (), s32[]{:S(2)}) async-start(), calls=%async_computation.5 | async-start | bytes 4325376 | tf_op jit(solution)/shard_map/all_gather | solution.py:100
  19.4 0.6 copy-start.6
  21.7 8.5 %copy-start.7 = (f32[32,2,8]{2,1,0:T(2,128)}, f32[32,2,8]{2,1,0:T(2,128)S(1)}, u32[]{:S(2)}) copy-start(f32[32,2,8]{2,1,0:T(2,128)S(1)} %copy.60) | copy-start | bytes 6148
  43.5 1.9 copy-start.4
  43.5 1.9 copy-start.5
  43.5 1.9 copy-start.9
  45.3 1.3 copy-start.2
  45.3 1.0 copy-start.1
  45.4 1.3 copy-start.10
  45.4 3.0 copy-start.8
  45.4 3.1 copy-start.11
  45.8 1.7 copy-start.3
  47.6 128.3 %all-gather.3.cloned.1.call-start = ((), (), s32[]{:S(2)}) async-start(), calls=%async_computation.3 | async-start | bytes 4325376 | tf_op jit(solution)/shard_map/all_gather | solution.py:100
  48.3 269.3 %reduce-scatter.5.cloned.1.call-start = ((), (), s32[]{:S(2)}) async-start(), calls=%async_computation.6 | async-start | bytes 4325376 | tf_op jit(solution)/shard_map/reduce_scatter | solution.py:103
  133.1 323.5 %reduce-scatter.3.cloned.1.call-start = ((), (), s32[]{:S(2)}) async-start(), calls=%async_computation.4 | async-start | bytes 4325376 | tf_op jit(solution)/shard_map/reduce_scatter | solution.py:103
  196.4 0.7 copy-start.12
Sparse Core Ops, SparseCore 0:
  47.7 64.6 all-gather.4
  115.3 60.5 all-gather.2
  178.2 139.4 reduce-scatter.4
  319.8 136.7 reduce-scatter.2
where the time goes:
time: 466 us; the launch traced here: 465 us
  waiting for transfers between devices  352 us (76%)
  matrix products  51.6 us (11%)
  local copies, waits for them, and re-layouts  27.3 us (6%)
  blocking collectives  14.3 us (3%)
  between operations  13.3 us (3%)
  other arithmetic  6.58 us (1%)
    reduce_scatter x2, waiting for transfers between devices, on_device(): mixture = lax.psum_scatter(partial, 'ex', scatter_dimension=0, tiled=True)  260 us
    all_gather x2, waiting for transfers between devices, on_device(): gathered = lax.all_gather(normed, 'ex', axis=0, tiled=True)  91.5 us
    dot_general x2, matrix products, expert_rows(): jnp.dot(hidden, down_proj[0], preferred_element_type=jnp.float32)  24.8 us
    dot_general x2, matrix products, expert_rows(): upper = jnp.dot(flat, up_proj[0], preferred_element_type=jnp.float32)  16.4 us
    all_to_all x1, blocking collectives, on_device(): mine = lax.all_to_all(table, 'ex', split_axis=2, concat_axis=1, tiled=True)  14.3 us
  transfers between devices with their start and end apart: 4, of which 4 were waited for; matrix products, arithmetic and copies ran while one was open for 9% of the time, Pallas kernels for 0%

commit v1 on v0

--- a/solution.py
+++ b/solution.py
@@ -97,7 +97,15 @@
             lengths[micro],
             norm_gain,
         )
-        gathered = lax.all_gather(normed, "ex", axis=0, tiled=True)
+        ways, here = (lax.axis_size("ex"), lax.axis_index("ex"))
+        grown, reach = (normed, 1)
+        while reach < ways:
+            theirs = lax.ppermute(grown, "ex", [(d, d ^ reach) for d in range(ways)])
+            mine_first = jnp.concatenate([grown, theirs], axis=0)
+            theirs_first = jnp.concatenate([theirs, grown], axis=0)
+            grown = jnp.where(here & reach == 0, mine_first, theirs_first)
+            reach = 2 * reach
+        gathered = grown
         out = expert_rows(gathered, gate_proj, up_proj, down_proj)
         partial = (mine[micro] * out.astype(jnp.float32)).astype(jnp.bfloat16)
         mixture = lax.psum_scatter(partial, "ex", scatter_dimension=0, tiled=True)

time: 466 us -> 566 us (1.21)
  waiting for transfers between devices: 352 us -> 415 us
  starting transfers between devices: 0.3 us -> 20 us
  other arithmetic: 6.58 us -> 23.7 us
  blocking collectives: 14.3 us -> 0 us
  matrix products: 51.6 us -> 58.8 us
  local copies, waits for them, and re-layouts: 27.3 us -> 33.4 us
    ppermute x0 -> x10, waiting for transfers between devices: none -> 193 us  [on_device(): theirs = lax.ppermute(grown, 'ex', [(d, d ^ reach) for d in range(ways)])]
    reduce_scatter x2, waiting for transfers between devices: 260 us -> 141 us  [on_device(): mixture = lax.psum_scatter(partial, 'ex', scatter_dimension=0, tiled=True)]
    all_gather x2 -> x0, waiting for transfers between devices: 91.5 us -> none  [on_device(): gathered = lax.all_gather(normed, 'ex', axis=0, tiled=True)]
    all_to_all x0 -> x1, waiting for transfers between devices: none -> 80.5 us  [on_device(): mine = lax.all_to_all(table, 'ex', split_axis=2, concat_axis=1, tiled=True)]
    ppermute x0 -> x10, starting transfers between devices: none -> 15.6 us  [on_device(): theirs = lax.ppermute(grown, 'ex', [(d, d ^ reach) for d in range(ways)])]
    select_n x0 -> x8, other arithmetic: none -> 14.6 us  [on_device(): grown = jnp.where(here & reach == 0, mine_first, theirs_first)]
    all_to_all x1 -> x0, blocking collectives: 14.3 us -> none  [on_device(): mine = lax.all_to_all(table, 'ex', split_axis=2, concat_axis=1, tiled=True)]
  transfers between devices with their start and end apart: 4 -> 13, of which waited for: 4 -> 11; matrix products, arithmetic and copies ran while one was open for 9% -> 6% of each run, Pallas kernels for 0% -> 0%
where the time goes in v1:
time: 566 us; the launch traced here: 564 us
  waiting for transfers between devices  415 us (73%)
  matrix products  58.8 us (10%)
  local copies, waits for them, and re-layouts  33.4 us (6%)
  other arithmetic  23.7 us (4%)
  starting transfers between devices  20 us (4%)
  between operations  13.6 us (2%)
    ppermute x10, waiting for transfers between devices, on_device(): theirs = lax.ppermute(grown, 'ex', [(d, d ^ reach) for d in range(ways)])  193 us
    reduce_scatter x2, waiting for transfers between devices, on_device(): mixture = lax.psum_scatter(partial, 'ex', scatter_dimension=0, tiled=True)  141 us
    all_to_all x1, waiting for transfers between devices, on_device(): mine = lax.all_to_all(table, 'ex', split_axis=2, concat_axis=1, tiled=True)  80.5 us
    dot_general x2, matrix products, expert_rows(): jnp.dot(hidden, down_proj[0], preferred_element_type=jnp.float32)  29.2 us
    dot_general x2, matrix products, expert_rows(): upper = jnp.dot(flat, up_proj[0], preferred_element_type=jnp.float32)  19.1 us
    ppermute x10, starting transfers between devices, on_device(): theirs = lax.ppermute(grown, 'ex', [(d, d ^ reach) for d in range(ways)])  15.6 us
    select_n x8, other arithmetic, on_device(): grown = jnp.where(here & reach == 0, mine_first, theirs_first)  14.6 us
  transfers between devices with their start and end apart: 13, of which 11 were waited for; matrix products, arithmetic and copies ran while one was open for 6% of the time, Pallas kernels for 0%

profile of v1, /device:TPU:0, one launch (start us, length us, event | category | flops | bytes accessed | tf_op | source)
XLA Modules:
  0.0 564.1 jit_solution(7220497137164362956)
XLA Ops:
  9.2 3.1 fusion.62
  12.3 2.2 reshape_squeeze.29
  14.5 2.6 fusion.65
  25.0 3.1 fusion.63
  28.1 2.2 reshape_squeeze.31
  31.2 2.2 reshape_squeeze.25
  35.0 3.2 fusion.64
  41.4 2.2 reshape_squeeze.27
  43.6 1.8 fusion.25
  49.4 1.9 maximum_select_fusion.15
  51.3 2.8 collective-permute-start.6
  54.1 6.9 %collective-permute-done.6 = bf16[64,2048]{1,0:T(8,128)(2,1)} collective-permute-done((bf16[64,2048]{1,0:T(8,128)(2,1)}, bf16[64,2048]{1,0:T(8,128)(2,1)}, u32[]{:S(2)}, u32[]{:S(2)}) %collective-permute-start.6) | collective-permute-done | bytes 262176 | tf_op jit(solution)/shard_map/ppermute | solution.py:103
  61.0 2.2 maximum_select_fusion.13
  65.0 12.0 %collective-permute-done.7 = bf16[128,2048]{1,0:T(8,128)(2,1)} collective-permute-done((bf16[128,2048]{1,0:T(8,128)(2,1)}, bf16[128,2048]{1,0:T(8,128)(2,1)}, u32[]{:S(2)}, u32[]{:S(2)}) %collective-permute-start.7) | collective-permute-done | bytes 524320 | tf_op jit(solution)/shard_map/ppermute | solution.py:103
  77.0 2.9 maximum_select_fusion.5
  81.4 22.6 %collective-permute-done.8 = bf16[256,2048]{1,0:T(8,128)(2,1)} collective-permute-done((bf16[256,2048]{1,0:T(8,128)(2,1)}, bf16[256,2048]{1,0:T(8,128)(2,1)}, u32[]{:S(2)}, u32[]{:S(2)}) %collective-permute-start.8) | collective-permute-done | bytes 1048608 | tf_op jit(solution)/shard_map/ppermute | solution.py:103
  104.0 4.7 maximum_select_fusion.3
  108.7 2.2 collective-permute-start.9
  117.3 4.0 all-to-all-start
  121.5 80.5 %all-to-all-done = f32[2,32,32]{1,0,2:T(2,128)} async-done(((f32[2,32,32]{1,0,2:T(2,128)}), f32[2,32,32]{1,0,2:T(2,128)}, u32[]{:S(2)}, u32[]{:S(2)}) %all-to-all-start) | async-done | bytes 8224 | tf_op jit(solution)/shard_map/all_to_all | solution.py:88
  204.9 9.4 %fusion.2 = f32[1024,768]{1,0:T(8,128)} fusion(bf16[1,2048,768]{2,1,0:T(8,128)(2,1)} %param.24, bf16[512,2048]{1,0:T(8,128)(2,1)} %collective-permute-done.9, bf16[512,2048]{1,0:T(8,128)(2,1)} %maximum_select_fusion.3, pred[]{:T(512)S(6)} %eq.60), kind=kOutput, calls=%fused_computation.6 | convolution fusion | flops 3240099840 | bytes 10485761 | tf_op jit(solution)/shard_map/dot_general | solution.py:64
  214.4 14.6 %multiply_convert_fusion = bf16[1024,2048]{1,0:T(8,128)(2,1)} fusion(f32[1024]{0:T(1024)} %mul.109, bf16[1,768,2048]{2,1,0:T(8,128)(2,1)S(1)} %copy-done, f32[1024,768]{1,0:T(8,128)} %fusion.2, bf16[1,2048,768]{2,1,0:T(8,128)(2,1)} %param.23, bf16[512,2048]{1,0:T(8,128)(2,1)} %collective-permute-done.9, bf16[512,2048]{1,0:T(8,128)(2,1)} %maximum_select_fusion.3, ...), kind=kOutput, calls=%fused_computation | convolution fusion | flops 6474432512 | bytes 17829888 | tf_op jit(solution)/shard_map/dot_general | solution.py:66
  231.3 10.6 %collective-permute-done.1 = bf16[64,2048]{1,0:T(8,128)(2,1)S(1)} collective-permute-done((bf16[64,2048]{1,0:T(8,128)(2,1)S(1)}, bf16[64,2048]{1,0:T(8,128)(2,1)S(1)}, u32[]{:S(2)}, u32[]{:S(2)}) %collective-permute-start.1) | collective-permute-done | bytes 262176 | tf_op jit(solution)/shard_map/ppermute | solution.py:103
  242.1 13.6 %collective-permute-done.2 = bf16[128,2048]{1,0:T(8,128)(2,1)S(1)} collective-permute-done((bf16[128,2048]{1,0:T(8,128)(2,1)S(1)}, bf16[128,2048]{1,0:T(8,128)(2,1)S(1)}, u32[]{:S(2)}, u32[]{:S(2)}) %collective-permute-start.2) | collective-permute-done | bytes 524320 | tf_op jit(solution)/shard_map/ppermute | solution.py:103
  257.2 26.3 %collective-permute-done.3 = bf16[256,2048]{1,0:T(8,128)(2,1)S(1)} collective-permute-done((bf16[256,2048]{1,0:T(8,128)(2,1)S(1)}, bf16[256,2048]{1,0:T(8,128)(2,1)S(1)}, u32[]{:S(2)}, u32[]{:S(2)}) %collective-permute-start.3) | collective-permute-done | bytes 1048608 | tf_op jit(solution)/shard_map/ppermute | solution.py:103
  283.5 2.5 maximum_select_fusion.2
  286.0 4.9 collective-permute-start.4
  291.0 97.9 %collective-permute-done.4 = bf16[512,2048]{1,0:T(8,128)(2,1)} collective-permute-done((bf16[512,2048]{1,0:T(8,128)(2,1)}, bf16[512,2048]{1,0:T(8,128)(2,1)}, u32[]{:S(2)}, u32[]{:S(2)}) %collective-permute-start.4) | collective-permute-done | bytes 2097184 | tf_op jit(solution)/shard_map/ppermute | solution.py:103
  388.9 9.6 %fusion.4 = f32[1024,768]{1,0:T(8,128)} fusion(bf16[1,2048,768]{2,1,0:T(8,128)(2,1)} %param.24, bf16[512,2048]{1,0:T(8,128)(2,1)} %collective-permute-done.4, bf16[512,2048]{1,0:T(8,128)(2,1)} %maximum_select_fusion.2, pred[]{:T(512)S(6)} %eq.60), kind=kOutput, calls=%fused_computation.8 | convolution fusion | flops 3240099840 | bytes 10485761 | tf_op jit(solution)/shard_map/dot_general | solution.py:64
  398.5 14.6 %multiply_convert_fusion.1 = bf16[1024,2048]{1,0:T(8,128)(2,1)} fusion(f32[1024]{0:T(1024)S(1)} %mul.96, bf16[1,768,2048]{2,1,0:T(8,128)(2,1)S(1)} %copy-done, f32[1024,768]{1,0:T(8,128)} %fusion.4, bf16[1,2048,768]{2,1,0:T(8,128)(2,1)} %param.23, bf16[512,2048]{1,0:T(8,128)(2,1)} %collective-permute-done.4, bf16[512,2048]{1,0:T(8,128)(2,1)} %maximum_select_fusion.2, ...), kind=kOutput, calls=%fused_computation.1 | convolution fusion | flops 6474432512 | bytes 17829888 | tf_op jit(solution)/shard_map/dot_general | solution.py:66
  413.8 141.4 %reduce-scatter.3.cloned.1.call-done = bf16[32,2048]{1,0:T(8,128)(2,1)} async-done(((bf16[1024,2048]{1,0:T(8,128)(2,1)}), bf16[32,2048]{1,0:T(8,128)(2,1)}) %reduce-scatter.3.cloned.1.call-update) | async-done | bytes 131088 | tf_op jit(solution)/shard_map/reduce_scatter | solution.py:111
  555.2 2.1 fusion.33
  (85 shorter events, 37.7 us)
Async XLA Ops:
  6.5 207.8 %copy-start = (bf16[1,768,2048]{2,1,0:T(8,128)(2,1)S(1)}, bf16[1,768,2048]{2,1,0:T(8,128)(2,1)}, u32[]{:S(2)}) copy-start(bf16[1,768,2048]{2,1,0:T(8,128)(2,1)} %param.25) | copy-start | bytes 9437188
  19.4 0.6 copy-start.6
  21.7 8.5 %copy-start.7 = (f32[32,2,8]{2,1,0:T(2,128)}, f32[32,2,8]{2,1,0:T(2,128)S(1)}, u32[]{:S(2)}) copy-start(f32[32,2,8]{2,1,0:T(2,128)S(1)} %copy.60) | copy-start | bytes 6148
  43.6 1.9 copy-start.4
  43.6 1.9 copy-start.5
  43.6 1.9 copy-start.9
  45.4 1.3 copy-start.2
  45.4 1.0 copy-start.1
  45.5 1.3 copy-start.10
  45.9 1.7 copy-start.3
  47.6 1.8 collective-permute-start.5
  51.3 9.8 %collective-permute-start.6 = (bf16[64,2048]{1,0:T(8,128)(2,1)}, bf16[64,2048]{1,0:T(8,128)(2,1)}, u32[]{:S(2)}, u32[]{:S(2)}) collective-permute-start(bf16[64,2048]{1,0:T(8,128)(2,1)} %maximum_select_fusion.15), channel_id=1, source_target_pairs={{0,2},{1,3},{2,0},{3,1},{4,6},{5,7},{6,4},{7,5},{8,10},{9,11},{10,... | collective-permute-start | bytes 786440 | tf_op jit(solution)/shard_map/ppermute | solution.py:103
  63.2 13.8 %collective-permute-start.7 = (bf16[128,2048]{1,0:T(8,128)(2,1)}, bf16[128,2048]{1,0:T(8,128)(2,1)}, u32[]{:S(2)}, u32[]{:S(2)}) collective-permute-start(bf16[128,2048]{1,0:T(8,128)(2,1)} %maximum_select_fusion.13), channel_id=1, source_target_pairs={{0,4},{1,5},{2,6},{3,7},{4,0},{5,1},{6,2},{7,3},{8,12},{9,13},{10,... | collective-permute-start | bytes 1572872 | tf_op jit(solution)/shard_map/ppermute | solution.py:103
  65.0 45.9 %copy-start.8 = (f32[2,32,8]{1,2,0:T(8,128)S(1)}, f32[2,32,8]{1,2,0:T(8,128)}, u32[]{:S(2)}) copy-start(f32[2,32,8]{1,2,0:T(8,128)} %param.21) | copy-start | bytes 6148
  79.9 24.1 %collective-permute-start.8 = (bf16[256,2048]{1,0:T(8,128)(2,1)}, bf16[256,2048]{1,0:T(8,128)(2,1)}, u32[]{:S(2)}, u32[]{:S(2)}) collective-permute-start(bf16[256,2048]{1,0:T(8,128)(2,1)} %maximum_select_fusion.5), channel_id=1, source_target_pairs={{0,8},{1,9},{2,10},{3,11},{4,12},{5,13},{6,14},{7,15},{8,0},{9,1},... | collective-permute-start | bytes 3145736 | tf_op jit(solution)/shard_map/ppermute | solution.py:103
  108.7 96.2 %collective-permute-start.9 = (bf16[512,2048]{1,0:T(8,128)(2,1)}, bf16[512,2048]{1,0:T(8,128)(2,1)}, u32[]{:S(2)}, u32[]{:S(2)}) collective-permute-start(bf16[512,2048]{1,0:T(8,128)(2,1)} %maximum_select_fusion.3), channel_id=1, source_target_pairs={{0,16},{1,17},{2,18},{3,19},{4,20},{5,21},{6,22},{7,23},{8,24},{9,... | collective-permute-start | bytes 6291464 | tf_op jit(solution)/shard_map/ppermute | solution.py:103
  117.3 84.7 %all-to-all-start = ((f32[2,32,32]{1,0,2:T(2,128)}), f32[2,32,32]{1,0,2:T(2,128)}, u32[]{:S(2)}, u32[]{:S(2)}) async-start(f32[2,32,32]{1,0,2:T(2,128)} %copy.57), calls=%async_computation | async-start | bytes 65536 | tf_op jit(solution)/shard_map/all_to_all | solution.py:88
  121.2 292.6 %reduce-scatter.5.cloned.1.call-start = ((), (), s32[]{:S(2)}) async-start(), calls=%async_computation.4 | async-start | bytes 4325376 | tf_op jit(solution)/shard_map/reduce_scatter | solution.py:111
  229.0 326.2 %reduce-scatter.3.cloned.1.call-start = ((), (), s32[]{:S(2)}) async-start(), calls=%async_computation.3 | async-start | bytes 4325376 | tf_op jit(solution)/shard_map/reduce_scatter | solution.py:111
  229.2 1.4 collective-permute-start
  230.7 11.2 %collective-permute-start.1 = (bf16[64,2048]{1,0:T(8,128)(2,1)S(1)}, bf16[64,2048]{1,0:T(8,128)(2,1)S(1)}, u32[]{:S(2)}, u32[]{:S(2)}) collective-permute-start(bf16[64,2048]{1,0:T(8,128)(2,1)S(1)} %maximum_select_fusion.14), channel_id=1, source_target_pairs={{0,2},{1,3},{2,0},{3,1},{4,6},{5,7},{6,4},{7,5},{8,10},{9,11},{10,... | collective-permute-start | bytes 786440 | tf_op jit(solution)/shard_map/ppermute | solution.py:103
  242.0 13.7 %collective-permute-start.2 = (bf16[128,2048]{1,0:T(8,128)(2,1)S(1)}, bf16[128,2048]{1,0:T(8,128)(2,1)S(1)}, u32[]{:S(2)}, u32[]{:S(2)}) collective-permute-start(bf16[128,2048]{1,0:T(8,128)(2,1)S(1)} %maximum_select_fusion.12), channel_id=1, source_target_pairs={{0,4},{1,5},{2,6},{3,7},{4,0},{5,1},{6,2},{7,3},{8,12},{9,13},{10,... | collective-permute-start | bytes 1572872 | tf_op jit(solution)/shard_map/ppermute | solution.py:103
  256.0 27.5 %collective-permute-start.3 = (bf16[256,2048]{1,0:T(8,128)(2,1)S(1)}, bf16[256,2048]{1,0:T(8,128)(2,1)S(1)}, u32[]{:S(2)}, u32[]{:S(2)}) collective-permute-start(bf16[256,2048]{1,0:T(8,128)(2,1)S(1)} %maximum_select_fusion.4), channel_id=1, source_target_pairs={{0,8},{1,9},{2,10},{3,11},{4,12},{5,13},{6,14},{7,15},{8,0},{9,1},... | collective-permute-start | bytes 3145736 | tf_op jit(solution)/shard_map/ppermute | solution.py:103
  286.0 102.8 %collective-permute-start.4 = (bf16[512,2048]{1,0:T(8,128)(2,1)}, bf16[512,2048]{1,0:T(8,128)(2,1)}, u32[]{:S(2)}, u32[]{:S(2)}) collective-permute-start(bf16[512,2048]{1,0:T(8,128)(2,1)} %maximum_select_fusion.2), channel_id=1, source_target_pairs={{0,16},{1,17},{2,18},{3,19},{4,20},{5,21},{6,22},{7,23},{8,24},{9,... | collective-permute-start | bytes 6291464 | tf_op jit(solution)/shard_map/ppermute | solution.py:103
  413.1 0.7 copy-start.11
Sparse Core Ops, SparseCore 0:
  229.1 148.1 reduce-scatter.4
  413.2 141.9 reduce-scatter.2
